TPU v7x, 256 devices: a whole 4x4x8 slice. The times are simulated.
256 devices in a mesh: wide: 64 (over y, z, core), narrow: 4 (over x).
Axes of the slice: x: 4, y: 4, z: 8, core: 2. Of those that a mesh axis runs over, the one named last changes fastest.
Arguments:
- patches: bfloat16 [65536, 1280], P('wide', 'narrow'), may hold values from -6 to 6
- norm_gain: float32 [1280], replicated, may hold values from 0.1 to 1.9
- norm_bias: float32 [1280], replicated, may hold values from -3 to 3
- w_in: bfloat16 [1280, 5120], P('wide', 'narrow'), may hold values from -0.15625 to 0.15625
- b_in: float32 [5120], P('narrow'), may hold values from -3 to 3
- w_out: bfloat16 [5120, 1280], P('narrow', 'wide'), may hold values from -0.078125 to 0.078125
- b_out: float32 [1280], P('narrow'), may hold values from -3 to 3
- w_proj: bfloat16 [4, 1280, 1280], P(None, 'narrow', 'wide'), may hold values from -0.078125 to 0.078125
- b_proj: float32 [1280], P('narrow'), may hold values from -3 to 3
- text: bfloat16 [32768, 1280], P('wide', 'narrow'), may hold values from -6 to 6
- place: int32 [16384], replicated, may hold values from -1 to 32767, as said below
Outputs:
- prompt_embeds: bfloat16 [32768, 1280], P('wide', 'narrow')
Inputs may be any that keep to these rules, and one draw needn't show every extreme that they name: `place`: of the 256 entries of one wide index (entries i * 256 to (i + 1) * 256 - 1), the valid ones (>= 0) come first and -1 fills the rest; three quarters or more are valid, and all are valid for some wide index. Valid values are distinct. For one wide index, at most 8 valid entries v have the same v // 512, and every wide index reaches 8 for some value.
All inputs are finite; a program needn't handle non-finite values.
Results may differ from a plain program's by a relative error of at most 0.012.
Values may be sent and summed in bfloat16 or wider, within the bound.
A program may use at most 64 MiB of HBM per device.

v0:
```python
import jax
import jax.numpy as jnp
from jax import lax
from jax.sharding import PartitionSpec as P


def per_device(
    patches, norm_gain, norm_bias, w_in, b_in, w_out, b_out, w_proj, b_proj, text, place
):
    whole = lax.all_gather(patches, "narrow", axis=1, tiled=True)
    values = whole.astype(jnp.float32)
    center = jnp.mean(values, axis=-1, keepdims=True)
    spread = jnp.mean(jnp.square(values - center), axis=-1, keepdims=True)
    normed = ((values - center) * lax.rsqrt(spread + 1e-06) * norm_gain + norm_bias).astype(
        jnp.bfloat16
    )
    rows_in, cols_out, proj_cols = (
        lax.all_gather(w_in, "wide", axis=0, tiled=True),
        lax.all_gather(w_out, "wide", axis=1, tiled=True),
        lax.all_gather(w_proj, "wide", axis=2, tiled=True),
    )
    product = jnp.dot(normed, rows_in, preferred_element_type=jnp.float32)
    hidden = jax.nn.gelu(product + b_in, approximate=False).astype(jnp.bfloat16)
    partial_out = jnp.dot(hidden, cols_out, preferred_element_type=jnp.float32)
    mlp_out = lax.psum_scatter(
        partial_out.astype(jnp.bfloat16), "narrow", scatter_dimension=1, tiled=True
    ).astype(jnp.float32)
    stream = (patches.astype(jnp.float32) + (mlp_out + b_out)).astype(jnp.bfloat16)
    merge_count = stream.shape[0] // 4
    merged = stream.reshape(merge_count, 4 * stream.shape[1])
    groups = lax.axis_size("wide")
    own_index = lax.axis_index("wide")
    seq_rows = text.shape[0]
    bucket = seq_rows // groups
    place_table = place.reshape(groups, merge_count)
    owners = jnp.where(place_table >= 0, place_table // seq_rows, groups)
    own_owners = lax.dynamic_index_in_dim(owners, own_index, 0, keepdims=False)
    owner_hits = (own_owners[:, None] == jnp.arange(groups, dtype=jnp.int32)[None, :]).astype(
        jnp.int32
    )
    slot_out = jnp.sum(jnp.cumsum(owner_hits, axis=0) * owner_hits, axis=1) - 1
    slot_out = jnp.where(own_owners < groups, slot_out, bucket)
    arriving = owners == own_index
    slot_in = jnp.cumsum(arriving.astype(jnp.int32), axis=1) - 1
    slot_in = jnp.where(arriving, slot_in, bucket)
    local_row = jnp.where(arriving, place_table % seq_rows, seq_rows)
    source_ids = jnp.arange(groups, dtype=jnp.int32)[:, None]
    targets = (
        jnp.full((groups, bucket), seq_rows, jnp.int32)
        .at[source_ids, slot_in]
        .set(local_row, mode="drop")
    )
    partial_proj = jnp.dot(
        merged, proj_cols.reshape(-1, proj_cols.shape[2]), preferred_element_type=jnp.float32
    )
    vision = (
        lax.psum_scatter(
            partial_proj.astype(jnp.bfloat16), "narrow", scatter_dimension=1, tiled=True
        ).astype(jnp.float32)
        + b_proj
    ).astype(jnp.bfloat16)
    buffer = jnp.zeros((groups, bucket, vision.shape[1]), vision.dtype)
    received = lax.all_to_all(
        buffer.at[own_owners, slot_out].set(vision, mode="drop"),
        "wide",
        split_axis=0,
        concat_axis=0,
        tiled=True,
    )
    return text.at[targets.reshape(-1)].set(received.reshape(-1, received.shape[2]), mode="drop")


def solution(mesh):
    placed = (
        P("wide", "narrow"),
        P(),
        P(),
        P("wide", "narrow"),
        P("narrow"),
        P("narrow", "wide"),
        P("narrow"),
        P(None, "narrow", "wide"),
        P("narrow"),
        P("wide", "narrow"),
        P(),
    )
    return jax.shard_map(
        per_device, mesh=mesh, in_specs=placed, out_specs=P("wide", "narrow"), check_vma=False
    )
```

profile of v0, /device:TPU:1, one launch (start us, length us, event | category | flops | bytes accessed | tf_op | source)
XLA Modules:
  0.0 475.5 jit_solution(18074952579770676036)
XLA Ops:
  6.5 0.0 all-gather.7.cloned.1.call-start
  6.5 0.7 all-gather.7.cloned.1.call-update
  7.3 0.0 all-gather.13.cloned.1.call-start
  7.3 0.7 all-gather.13.cloned.1.call-update
  8.0 0.0 all-gather.11.cloned.1.call-start
  8.1 0.7 all-gather.11.cloned.1.call-update
  8.7 0.0 all-gather.9.cloned.1.call-start
  8.8 0.5 all-gather.9.cloned.1.call-update
  9.3 0.0 reduce-scatter.3.cloned.1.call-start
  9.4 41.4 %all-gather.7.cloned.1.call-done = bf16[1024,1280]{0,1:T(8,128)(2,1)} async-done(((bf16[1024,320]{0,1:T(8,128)(2,1)}), bf16[1024,1280]{0,1:T(8,128)(2,1)}) %all-gather.7.cloned.1.call-update) | async-done | bytes 2621456 | tf_op jit(solution)/shard_map/all_gather | solution.py:10
  50.7 2.3 convert_reduce_fusion
  53.1 0.2 copy-done
  53.2 0.7 fusion.2
  54.0 78.9 %all-gather.13.cloned.1.call-done = bf16[64,20,1280]{2,1,0:T(8,128)(2,1)} async-done(((bf16[1,20,1280]{2,1,0:T(8,128)(2,1)}), bf16[64,20,1280]{2,1,0:T(8,128)(2,1)}) %all-gather.13.cloned.1.call-update) | async-done | bytes 3276816 | tf_op jit(solution)/shard_map/all_gather | solution.py:19
  132.9 6.1 %reshape.317 = bf16[1280,1280]{1,0:T(8,128)(2,1)} reshape(bf16[64,20,1280]{2,1,0:T(8,128)(2,1)} %all-gather.13.cloned.1.call-done) | data formatting | bytes 6553600
  139.1 72.6 %all-gather.11.cloned.1.call-done = bf16[64,20,1280]{2,1,0:T(8,128)(2,1)} async-done(((bf16[1,20,1280]{2,1,0:T(8,128)(2,1)}), bf16[64,20,1280]{2,1,0:T(8,128)(2,1)}) %all-gather.11.cloned.1.call-update) | async-done | bytes 3276816 | tf_op jit(solution)/shard_map/all_gather | solution.py:18
  211.7 6.1 %reshape.315 = bf16[1280,1280]{1,0:T(8,128)(2,1)} reshape(bf16[64,20,1280]{2,1,0:T(8,128)(2,1)} %all-gather.11.cloned.1.call-done) | data formatting | bytes 6553600
  217.8 0.0 copy-done.6
  217.8 0.0 copy-done.7
  217.8 0.0 copy-done.8
  217.8 0.0 copy-start.1
  217.8 21.4 %convolution_convert_fusion = bf16[1024,1280]{0,1:T(8,128)(2,1)} fusion(bf16[1280,1280]{1,0:T(8,128)(2,1)} %reshape.317, bf16[1280,1280]{1,0:T(8,128)(2,1)} %reshape.315, bf16[1024,1280]{0,1:T(8,128)(2,1)S(1)} %copy-done, f32[1280]{0:T(1024)S(1)} %copy-done.6, f32[1280]{0:T(1024)S(1)} %copy-done.7, f32[1280]{0:T(1024)S(1)} %copy-done.8, ...), kind=kOutput, calls=%fused_computation.30 | convolution fusion | flops 6806568960 | bytes 11820032 | tf_op jit(solution)/shard_map/dot_general | solution.py:24
  239.2 0.0 reduce-scatter.3.cloned.1.call-update
  239.2 0.0 copy-start.2
  239.3 0.0 reduce-scatter.5.cloned.1.call-start
  239.3 0.0 copy-done.1
  239.4 0.1 fusion.40
  239.4 0.6 reduce-window.14
  240.0 0.2 slice_reduce_fusion.1
  240.3 0.1 add_add_fusion
  240.4 49.9 %all-gather.9.cloned.1.call-done = bf16[4,320,1280]{1,0,2:T(4,128)(2,1)} async-done(((bf16[4,320,20]{1,0,2:T(4,128)(2,1)}), bf16[4,320,1280]{1,0,2:T(4,128)(2,1)}) %all-gather.9.cloned.1.call-update) | async-done | bytes 3276816 | tf_op jit(solution)/shard_map/all_gather | solution.py:20
  290.3 7.3 %copy.46 = bf16[4,320,1280]{2,1,0:T(8,128)(2,1)S(1)} copy(bf16[4,320,1280]{1,0,2:T(4,128)(2,1)} %all-gather.9.cloned.1.call-done) | data formatting | bytes 6553600 | tf_op jit(solution)/shard_map/all_gather | solution.py:20
  297.6 28.3 %reduce-scatter.3.cloned.1.call-done = bf16[1024,320]{0,1:T(8,128)(2,1)} async-done(((bf16[1024,1280]{0,1:T(8,128)(2,1)}), bf16[1024,320]{0,1:T(8,128)(2,1)}) %reduce-scatter.3.cloned.1.call-update) | async-done | bytes 655376 | tf_op jit(solution)/shard_map/reduce_scatter | solution.py:25
  326.0 0.0 copy-done.2
  326.0 2.4 add_convert_fusion
  328.4 2.2 copy.45
  330.6 2.5 reshape.287
  333.1 3.3 convolution_convert_fusion.1
  336.4 0.0 reduce-scatter.5.cloned.1.call-update
  336.4 0.1 fusion.31
  336.5 1.2 copy.48
  337.7 0.1 copy.42
  337.8 0.1 sub.37
  337.9 0.6 reduce-window.16
  338.5 0.2 slice_reduce_fusion
  338.7 0.1 fusion.35
  338.9 0.1 compare_select_fusion
  338.9 20.6 %reduce-scatter.5.cloned.1.call-done = bf16[256,320]{0,1:T(8,128)(2,1)} async-done(((bf16[256,1280]{0,1:T(8,128)(2,1)}), bf16[256,320]{0,1:T(8,128)(2,1)}) %reduce-scatter.5.cloned.1.call-update) | async-done | bytes 163856 | tf_op jit(solution)/shard_map/reduce_scatter | solution.py:57
  359.5 0.0 copy-done.3
  359.5 1.0 add_convert_fusion.1
  360.5 0.2 copy.47
  360.7 0.8 broadcast_in_dim.47
  361.5 30.9 %scatter_fusion = bf16[64,8,320]{2,1,0:T(8,128)(2,1)} fusion(bf16[64,8,320]{2,1,0:T(8,128)(2,1)} %broadcast_in_dim.47, s32[256]{0:T(256)S(1)} %bitcast.42, bf16[256,320]{1,0:T(8,128)(2,1)S(1)} %copy.47), kind=kCustom, calls=%fused_computation | custom fusion | bytes 493568 | tf_op jit(solution)/shard_map/scatter | solution.py:64
  392.4 11.9 %all-to-all-start = ((bf16[64,8,320]{2,1,0:T(8,128)(2,1)}), bf16[64,8,320]{2,1,0:T(8,128)(2,1)S(1)}, u32[]{:S(2)}, u32[]{:S(2)}) async-start(bf16[64,8,320]{2,1,0:T(8,128)(2,1)} %scatter_fusion), calls=%async_computation.2 | async-start | bytes 786432 | tf_op jit(solution)/shard_map/all_to_all | solution.py:63
  404.3 0.0 copy-done.5
  404.3 0.1 multiply_reduce_fusion
  404.4 0.1 and_reduce_fusion
  404.6 60.3 %scatter_custom_fusion.2 = s32[512]{0:T(512)S(1)} fusion(s32[16384]{0:T(1024)S(1)} %bitcast.45, s32[16384]{0:T(1024)S(1)} %bitcast.46, s32[]{:T(128)} %constant.43.clone.1), kind=kCustom, calls=%fused_computation.95 | custom fusion | bytes 2052
  464.9 0.1 reshape.292
  465.0 0.1 copy.43
  465.0 0.1 reshape.285
  465.1 0.0 all-to-all-done
  465.2 2.6 scatter_custom_fusion.1
  467.7 0.9 copy.49
  (25 shorter events, 0.3 us)
Async XLA Ops:
  6.5 44.2 %all-gather.7.cloned.1.call-start = ((), (), s32[]{:S(2)}) async-start(), calls=%async_computation.3 | async-start | bytes 3276800 | tf_op jit(solution)/shard_map/all_gather | solution.py:10
  7.3 125.7 %all-gather.13.cloned.1.call-start = ((), (), s32[]{:S(2)}) async-start(), calls=%async_computation.8 | async-start | bytes 3993600 | tf_op jit(solution)/shard_map/all_gather | solution.py:19
  8.0 203.7 %all-gather.11.cloned.1.call-start = ((), (), s32[]{:S(2)}) async-start(), calls=%async_computation.7 | async-start | bytes 3993600 | tf_op jit(solution)/shard_map/all_gather | solution.py:18
  8.7 281.6 %all-gather.9.cloned.1.call-start = ((), (), s32[]{:S(2)}) async-start(), calls=%async_computation.5 | async-start | bytes 3993600 | tf_op jit(solution)/shard_map/all_gather | solution.py:20
  9.3 316.6 %reduce-scatter.3.cloned.1.call-start = ((), (), s32[]{:S(2)}) async-start(), calls=%async_computation.4 | async-start | bytes 3276800 | tf_op jit(solution)/shard_map/reduce_scatter | solution.py:25
  50.7 2.5 copy-start
  139.1 78.8 %copy-start.6 = (f32[1280]{0:T(1024)S(1)}, f32[1280]{0:T(1024)}, u32[]{:S(2)}) copy-start(f32[1280]{0:T(1024)} %param.15) | copy-start | bytes 15364
  139.1 78.8 %copy-start.7 = (f32[1280]{0:T(1024)S(1)}, f32[1280]{0:T(1024)}, u32[]{:S(2)}) copy-start(f32[1280]{0:T(1024)} %param.13) | copy-start | bytes 15364
  139.1 78.8 %copy-start.8 = (f32[1280]{0:T(1024)S(1)}, f32[1280]{0:T(1024)}, u32[]{:S(2)}) copy-start(f32[1280]{0:T(1024)} %param.12) | copy-start | bytes 15364
  217.8 21.5 %copy-start.1 = (s32[16384]{0:T(1024)S(1)}, s32[16384]{0:T(1024)}, u32[]{:S(2)}) copy-start(s32[16384]{0:T(1024)} %param.21) | copy-start | bytes 196612
  239.2 86.7 %copy-start.2 = (f32[320]{0:T(512)S(1)}, f32[320]{0:T(512)}, u32[]{:S(2)}) copy-start(f32[320]{0:T(512)} %param.17) | copy-start | bytes 3844
  239.3 120.2 %reduce-scatter.5.cloned.1.call-start = ((), (), s32[]{:S(2)}) async-start(), calls=%async_computation.6 | async-start | bytes 819200 | tf_op jit(solution)/shard_map/reduce_scatter | solution.py:57
  333.1 26.4 %copy-start.3 = (f32[320]{0:T(512)S(1)}, f32[320]{0:T(512)}, u32[]{:S(2)}) copy-start(f32[320]{0:T(512)} %param.19) | copy-start | bytes 3844
  336.4 67.9 %copy-start.5 = (s32[2]{0:T(128)S(1)}, s32[2]{0:T(128)}, u32[]{:S(2)}) copy-start(s32[2]{0:T(128)} %constant.137) | copy-start | bytes 28
  336.4 68.0 %copy-start.4 = (s32[2]{0:T(128)S(1)}, s32[2]{0:T(128)}, u32[]{:S(2)}) copy-start(s32[2]{0:T(128)} %constant.140) | copy-start | bytes 28
  392.4 72.8 %all-to-all-start = ((bf16[64,8,320]{2,1,0:T(8,128)(2,1)}), bf16[64,8,320]{2,1,0:T(8,128)(2,1)S(1)}, u32[]{:S(2)}, u32[]{:S(2)}) async-start(bf16[64,8,320]{2,1,0:T(8,128)(2,1)} %scatter_fusion), calls=%async_computation.2 | async-start | bytes 786432 | tf_op jit(solution)/shard_map/all_to_all | solution.py:63
Sparse Core Ops, SparseCore 0:
  9.2 41.5 all-gather.6
  53.4 79.4 all-gather.12
  135.6 76.0 all-gather.10
  214.3 75.9 all-gather.8
  292.7 33.2 reduce-scatter.2
  336.5 22.9 reduce-scatter.4
where the time goes:
time: 477 us; the launch traced here: 475 us
  waiting for transfers between devices  294 us (62%)
  local copies, waits for them, and re-layouts  122 us (26%)
  matrix products  24.7 us (5%)
  between operations  13.7 us (3%)
  starting transfers between devices  12.1 us (3%)
  other arithmetic  8.4 us (2%)
    all_gather x1, waiting for transfers between devices, per_device(): lax.all_gather(w_out, 'wide', axis=1, tiled=True)  78.9 us
    unnamed x25, local copies, waits for them, and re-layouts  74.1 us
    all_gather x1, waiting for transfers between devices, per_device(): lax.all_gather(w_in, 'wide', axis=0, tiled=True)  72.6 us
    all_gather x1, waiting for transfers between devices, per_device(): lax.all_gather(w_proj, 'wide', axis=2, tiled=True)  49.9 us
    all_gather x1, waiting for transfers between devices, per_device(): whole = lax.all_gather(patches, 'narrow', axis=1, tiled=True)  41.4 us
    scatter x1, local copies, waits for them, and re-layouts, per_device(): buffer.at[own_owners, slot_out].set(vision, mode='drop')  30.9 us
    reduce_scatter x1, waiting for transfers between devices, per_device(): lax.psum_scatter(partial_out.astype(jnp.bfloat16), 'narrow', scatter_dime...  28.3 us
    dot_general x1, matrix products, per_device(): partial_out = jnp.dot(hidden, cols_out, preferred_element_type=jnp.float32)  21.4 us
  transfers between devices with their start and end apart: 7, of which 6 were waited for; matrix products, arithmetic and copies ran while one was open for 23% of the time, Pallas kernels for 0%

commit v1 on v0

--- a/solution.py
+++ b/solution.py
@@ -4,10 +4,28 @@
 from jax.sharding import PartitionSpec as P
 
 
+def ring_gather(array, axis, dim):
+    ways, here, hop = (lax.axis_size(axis), lax.axis_index(axis), array.shape[dim])
+    lengths = [n * ways if d == dim else n for d, n in enumerate(array.shape)]
+    full = lax.dynamic_update_slice_in_dim(
+        jnp.zeros(lengths, array.dtype), array, here * hop, axis=dim
+    )
+    going_up = going_down = array
+    for far in range(1, ways // 2 + 1):
+        going_up = lax.ppermute(going_up, axis, [(d, (d + 1) % ways) for d in range(ways)])
+        full = lax.dynamic_update_slice_in_dim(full, going_up, (here - far) % ways * hop, axis=dim)
+        if 2 * far < ways:
+            going_down = lax.ppermute(going_down, axis, [(d, (d - 1) % ways) for d in range(ways)])
+            full = lax.dynamic_update_slice_in_dim(
+                full, going_down, (here + far) % ways * hop, axis=dim
+            )
+    return full
+
+
 def per_device(
     patches, norm_gain, norm_bias, w_in, b_in, w_out, b_out, w_proj, b_proj, text, place
 ):
-    whole = lax.all_gather(patches, "narrow", axis=1, tiled=True)
+    whole = ring_gather(patches, "narrow", 1)
     values = whole.astype(jnp.float32)
     center = jnp.mean(values, axis=-1, keepdims=True)
     spread = jnp.mean(jnp.square(values - center), axis=-1, keepdims=True)

time: 477 us -> 438 us (0.918)
  waiting for transfers between devices: 294 us -> 247 us
  starting transfers between devices: 12.1 us -> 17.5 us
    all_gather x1 -> x0, waiting for transfers between devices: 41.4 us -> none  [per_device(): whole = lax.all_gather(patches, 'narrow', axis=1, tiled=True)]
    ppermute x0 -> x3, waiting for transfers between devices: none -> 23.2 us  [the longest x2 23.2 us: ring_gather(): lax.ppermute(going_up, axis, [(d, (d + 1) % ways) for d in range(ways)])]
    all_gather x1, waiting for transfers between devices: 72.6 us -> 51.3 us  [per_device(): lax.all_gather(w_in, 'wide', axis=0, tiled=True)]
    all_gather x1, waiting for transfers between devices: 78.9 us -> 72.6 us  [per_device(): lax.all_gather(w_out, 'wide', axis=1, tiled=True)]
    ppermute x0 -> x3, starting transfers between devices: none -> 5.46 us  [the longest x2 4.1 us: ring_gather(): lax.ppermute(going_up, axis, [(d, (d + 1) % ways) for d in range(ways)])]
    unnamed x25 -> x29, local copies, waits for them, and re-layouts: 74.1 us -> 73.5 us
  transfers between devices with their start and end apart: 7 -> 9, of which waited for: 6 -> 7; matrix products, arithmetic and copies ran while one was open for 23% -> 25% of each run, Pallas kernels for 0% -> 0%
where the time goes in v1:
time: 438 us; the launch traced here: 436 us
  waiting for transfers between devices  247 us (56%)
  local copies, waits for them, and re-layouts  125 us (29%)
  matrix products  24.7 us (6%)
  starting transfers between devices  17.5 us (4%)
  between operations  13.5 us (3%)
  other arithmetic  7.2 us (2%)
    unnamed x29, local copies, waits for them, and re-layouts  73.5 us
    all_gather x1, waiting for transfers between devices, per_device(): lax.all_gather(w_out, 'wide', axis=1, tiled=True)  72.6 us
    all_gather x1, waiting for transfers between devices, per_device(): lax.all_gather(w_in, 'wide', axis=0, tiled=True)  51.3 us
    all_gather x1, waiting for transfers between devices, per_device(): lax.all_gather(w_proj, 'wide', axis=2, tiled=True)  49.5 us
    scatter x1, local copies, waits for them, and re-layouts, per_device(): buffer.at[own_owners, slot_out].set(vision, mode='drop')  30.9 us
    reduce_scatter x1, waiting for transfers between devices, per_device(): lax.psum_scatter(partial_out.astype(jnp.bfloat16), 'narrow', scatter_dime...  28.3 us
    ppermute x2, waiting for transfers between devices, ring_gather(): lax.ppermute(going_up, axis, [(d, (d + 1) % ways) for d in range(ways)])  23.2 us
    dot_general x1, matrix products, per_device(): partial_out = jnp.dot(hidden, cols_out, preferred_element_type=jnp.float32)  21.4 us
  transfers between devices with their start and end apart: 9, of which 7 were waited for; matrix products, arithmetic and copies ran while one was open for 25% of the time, Pallas kernels for 0%

profile of v1, /device:TPU:1, one launch (start us, length us, event | category | flops | bytes accessed | tf_op | source)
XLA Modules:
  0.0 435.8 jit_solution(3164539652179490823)
XLA Ops:
  6.5 0.7 all-gather.8.cloned.1.call-update
  7.3 0.0 all-gather.10.cloned.1.call-start
  7.3 0.7 all-gather.10.cloned.1.call-update
  8.0 0.0 all-gather.6.cloned.1.call-start
  8.1 2.1 collective-permute-start
  10.2 1.4 collective-permute-start.1
  11.5 12.3 %collective-permute-done = bf16[1024,320]{0,1:T(8,128)(2,1)S(1)} collective-permute-done((bf16[1024,320]{0,1:T(8,128)(2,1)}, bf16[1024,320]{0,1:T(8,128)(2,1)S(1)}, u32[]{:S(2)}, u32[]{:S(2)}) %collective-permute-start) | collective-permute-done | bytes 655392 | tf_op jit(solution)/shard_map/ppermute | solution.py:15
  23.8 2.0 collective-permute-start.2
  25.8 0.0 all-gather.6.cloned.1.call-update
  25.8 0.0 reduce-scatter.3.cloned.1.call-start
  25.9 0.3 broadcast_in_dim.52
  26.3 1.1 constant_dynamic-update-slice_fusion.3
  27.4 0.1 constant_dynamic-update-slice_fusion.2
  27.5 1.1 constant_dynamic-update-slice_fusion.1
  28.6 10.9 %collective-permute-done.2 = bf16[1024,320]{0,1:T(8,128)(2,1)} collective-permute-done((bf16[1024,320]{0,1:T(8,128)(2,1)S(1)}, bf16[1024,320]{0,1:T(8,128)(2,1)}, u32[]{:S(2)}, u32[]{:S(2)}) %collective-permute-start.2) | collective-permute-done | bytes 655392 | tf_op jit(solution)/shard_map/ppermute | solution.py:15
  39.6 1.1 constant_dynamic-update-slice_fusion
  40.7 0.5 convert_reduce_fusion
  41.2 0.7 fusion.2
  41.9 51.3 %all-gather.8.cloned.1.call-done = bf16[64,20,1280]{2,1,0:T(8,128)(2,1)} async-done(((bf16[1,20,1280]{2,1,0:T(8,128)(2,1)}), bf16[64,20,1280]{2,1,0:T(8,128)(2,1)}) %all-gather.8.cloned.1.call-update) | async-done | bytes 3276816 | tf_op jit(solution)/shard_map/all_gather | solution.py:36
  93.2 6.1 %reshape.315 = bf16[1280,1280]{1,0:T(8,128)(2,1)} reshape(bf16[64,20,1280]{2,1,0:T(8,128)(2,1)} %all-gather.8.cloned.1.call-done) | data formatting | bytes 6553600
  99.3 72.6 %all-gather.10.cloned.1.call-done = bf16[64,20,1280]{2,1,0:T(8,128)(2,1)} async-done(((bf16[1,20,1280]{2,1,0:T(8,128)(2,1)}), bf16[64,20,1280]{2,1,0:T(8,128)(2,1)}) %all-gather.10.cloned.1.call-update) | async-done | bytes 3276816 | tf_op jit(solution)/shard_map/all_gather | solution.py:37
  172.0 6.1 %reshape.317 = bf16[1280,1280]{1,0:T(8,128)(2,1)} reshape(bf16[64,20,1280]{2,1,0:T(8,128)(2,1)} %all-gather.10.cloned.1.call-done) | data formatting | bytes 6553600
  178.1 0.0 copy-start
  178.1 21.4 %convolution_convert_fusion = bf16[1024,1280]{0,1:T(8,128)(2,1)} fusion(bf16[1280,1280]{1,0:T(8,128)(2,1)} %reshape.317, bf16[1280,1280]{1,0:T(8,128)(2,1)} %reshape.315, bf16[1024,1280]{0,1:T(8,128)(2,1)S(1)} %constant_dynamic-update-slice_fusion, f32[1280]{0:T(1024)S(1)} %copy-done.8, f32[1280]{0:T(1024)S(1)} %copy-done.9, f32[1280]{0:T(1024)S(1)} %copy-done.10, ...), kind=kOutput, calls=%fused_computation.30 | convolution fusion | flops 6806568960 | bytes 11820032 | tf_op jit(solution)/shard_map/dot_general | solution.py:42
  199.5 0.0 reduce-scatter.3.cloned.1.call-update
  199.5 0.0 reduce-scatter.5.cloned.1.call-start
  199.6 0.0 copy-start.4
  199.7 0.1 fusion.31
  199.8 0.0 copy-start.2
  199.8 0.6 copy-done.2
  200.4 0.6 reduce-window.16
  201.0 0.2 slice_reduce_fusion
  201.2 49.5 %all-gather.6.cloned.1.call-done = bf16[4,320,1280]{1,0,2:T(4,128)(2,1)} async-done(((bf16[4,320,20]{1,0,2:T(4,128)(2,1)}), bf16[4,320,1280]{1,0,2:T(4,128)(2,1)}) %all-gather.6.cloned.1.call-update) | async-done | bytes 3276816 | tf_op jit(solution)/shard_map/all_gather | solution.py:38
  250.7 7.3 %copy.46 = bf16[4,320,1280]{2,1,0:T(8,128)(2,1)S(1)} copy(bf16[4,320,1280]{1,0,2:T(4,128)(2,1)} %all-gather.6.cloned.1.call-done) | data formatting | bytes 6553600 | tf_op jit(solution)/shard_map/all_gather | solution.py:38
  258.1 28.3 %reduce-scatter.3.cloned.1.call-done = bf16[1024,320]{0,1:T(8,128)(2,1)} async-done(((bf16[1024,1280]{0,1:T(8,128)(2,1)}), bf16[1024,320]{0,1:T(8,128)(2,1)}) %reduce-scatter.3.cloned.1.call-update) | async-done | bytes 655376 | tf_op jit(solution)/shard_map/reduce_scatter | solution.py:43
  286.4 2.4 add_convert_fusion
  288.8 2.2 copy.45
  291.0 2.5 reshape.287
  293.6 3.3 convolution_convert_fusion.1
  296.9 0.0 reduce-scatter.5.cloned.1.call-update
  296.9 0.1 fusion.40
  296.9 0.6 reduce-window.14
  297.6 0.2 slice_reduce_fusion.1
  297.8 0.1 add_add_fusion
  297.9 0.1 copy.42
  297.9 0.1 sub.43
  298.0 0.1 fusion.35
  298.1 0.7 or_select_fusion
  298.8 0.1 compare_select_fusion
  298.9 21.0 %reduce-scatter.5.cloned.1.call-done = bf16[256,320]{0,1:T(8,128)(2,1)} async-done(((bf16[256,1280]{0,1:T(8,128)(2,1)}), bf16[256,320]{0,1:T(8,128)(2,1)}) %reduce-scatter.5.cloned.1.call-update) | async-done | bytes 163856 | tf_op jit(solution)/shard_map/reduce_scatter | solution.py:75
  319.9 1.0 add_convert_fusion.1
  321.0 0.2 copy.47
  321.1 0.8 broadcast_in_dim.50
  321.9 30.9 %scatter_fusion = bf16[64,8,320]{2,1,0:T(8,128)(2,1)} fusion(bf16[64,8,320]{2,1,0:T(8,128)(2,1)} %broadcast_in_dim.50, s32[256]{0:T(256)S(1)} %bitcast.42, bf16[256,320]{1,0:T(8,128)(2,1)S(1)} %copy.47), kind=kCustom, calls=%fused_computation | custom fusion | bytes 493568 | tf_op jit(solution)/shard_map/scatter | solution.py:82
  352.8 11.9 %all-to-all-start = ((bf16[64,8,320]{2,1,0:T(8,128)(2,1)}), bf16[64,8,320]{2,1,0:T(8,128)(2,1)S(1)}, u32[]{:S(2)}, u32[]{:S(2)}) async-start(bf16[64,8,320]{2,1,0:T(8,128)(2,1)} %scatter_fusion), calls=%async_computation.2 | async-start | bytes 786432 | tf_op jit(solution)/shard_map/all_to_all | solution.py:81
  364.7 0.1 multiply_reduce_fusion
  364.8 0.1 and_reduce_fusion
  365.0 60.3 %scatter_custom_fusion.2 = s32[512]{0:T(512)S(1)} fusion(s32[16384]{0:T(1024)S(1)} %bitcast.45, s32[16384]{0:T(1024)S(1)} %bitcast.46, s32[]{:T(128)} %constant.49.clone.1), kind=kCustom, calls=%fused_computation.100 | custom fusion | bytes 2052
  425.3 0.1 reshape.292
  425.4 0.1 copy.43
  425.5 0.1 reshape.285
  425.6 0.2 copy.48
  425.8 2.6 scatter_custom_fusion.1
  428.4 0.9 copy.49
  (38 shorter events, 0.3 us)
Async XLA Ops:
  6.5 86.7 %all-gather.8.cloned.1.call-start = ((), (), s32[]{:S(2)}) async-start(), calls=%async_computation.6 | async-start | bytes 3993600 | tf_op jit(solution)/shard_map/all_gather | solution.py:36
  7.3 164.7 %all-gather.10.cloned.1.call-start = ((), (), s32[]{:S(2)}) async-start(), calls=%async_computation.7 | async-start | bytes 3993600 | tf_op jit(solution)/shard_map/all_gather | solution.py:37
  8.0 242.7 %all-gather.6.cloned.1.call-start = ((), (), s32[]{:S(2)}) async-start(), calls=%async_computation.4 | async-start | bytes 3993600 | tf_op jit(solution)/shard_map/all_gather | solution.py:38
  8.1 15.8 %collective-permute-start = (bf16[1024,320]{0,1:T(8,128)(2,1)}, bf16[1024,320]{0,1:T(8,128)(2,1)S(1)}, u32[]{:S(2)}, u32[]{:S(2)}) collective-permute-start(bf16[1024,320]{0,1:T(8,128)(2,1)} %param.11), channel_id=1, source_target_pairs={{0,1},{1,2},{2,3},{3,0},{4,5},{5,6},{6,7},{7,4},{8,9},{9,10},{10,1... | collective-permute-start | bytes 1966088 | tf_op jit(solution)/shard_map/ppermute | solution.py:15
  10.2 17.3 %collective-permute-start.1 = (bf16[1024,320]{0,1:T(8,128)(2,1)}, bf16[1024,320]{0,1:T(8,128)(2,1)}, u32[]{:S(2)}, u32[]{:S(2)}) collective-permute-start(bf16[1024,320]{0,1:T(8,128)(2,1)} %param.11), channel_id=1, source_target_pairs={{0,3},{1,0},{2,1},{3,2},{4,7},{5,4},{6,5},{7,6},{8,11},{9,8},{10,9... | collective-permute-start | bytes 1966088 | tf_op jit(solution)/shard_map/ppermute | solution.py:18
  23.8 15.7 %collective-permute-start.2 = (bf16[1024,320]{0,1:T(8,128)(2,1)S(1)}, bf16[1024,320]{0,1:T(8,128)(2,1)}, u32[]{:S(2)}, u32[]{:S(2)}) collective-permute-start(bf16[1024,320]{0,1:T(8,128)(2,1)S(1)} %collective-permute-done), channel_id=1, source_target_pairs={{0,1},{1,2},{2,3},{3,0},{4,5},{5,6},{6,7},{7,4},{8,9},{9,10},{10,1... | collective-permute-start | bytes 1966088 | tf_op jit(solution)/shard_map/ppermute | solution.py:15
  25.8 260.6 %reduce-scatter.3.cloned.1.call-start = ((), (), s32[]{:S(2)}) async-start(), calls=%async_computation.3 | async-start | bytes 3276800 | tf_op jit(solution)/shard_map/reduce_scatter | solution.py:43
  99.3 78.7 %copy-start.8 = (f32[1280]{0:T(1024)S(1)}, f32[1280]{0:T(1024)}, u32[]{:S(2)}) copy-start(f32[1280]{0:T(1024)} %param.15) | copy-start | bytes 15364
  99.3 78.7 %copy-start.9 = (f32[1280]{0:T(1024)S(1)}, f32[1280]{0:T(1024)}, u32[]{:S(2)}) copy-start(f32[1280]{0:T(1024)} %param.13) | copy-start | bytes 15364
  99.3 78.7 %copy-start.10 = (f32[1280]{0:T(1024)S(1)}, f32[1280]{0:T(1024)}, u32[]{:S(2)}) copy-start(f32[1280]{0:T(1024)} %param.12) | copy-start | bytes 15364
  178.1 21.5 %copy-start = (s32[16384]{0:T(1024)S(1)}, s32[16384]{0:T(1024)}, u32[]{:S(2)}) copy-start(s32[16384]{0:T(1024)} %param.21) | copy-start | bytes 196612
  199.5 120.4 %reduce-scatter.5.cloned.1.call-start = ((), (), s32[]{:S(2)}) async-start(), calls=%async_computation.5 | async-start | bytes 819200 | tf_op jit(solution)/shard_map/reduce_scatter | solution.py:75
  199.6 86.8 %copy-start.4 = (f32[320]{0:T(512)S(1)}, f32[320]{0:T(512)}, u32[]{:S(2)}) copy-start(f32[320]{0:T(512)} %param.17) | copy-start | bytes 3844
  199.8 0.6 copy-start.2
  201.2 87.6 %copy-start.3 = (s32[64,3]{0,1:T(4,128)}, s32[64,3]{0,1:T(4,128)S(1)}, u32[]{:S(2)}) copy-start(s32[64,3]{0,1:T(4,128)S(1)} %reduce-window.19) | copy-start | bytes 2308
  291.0 7.0 %slice-start = ((s32[64,3]{0,1:T(4,128)}), s32[64,2]{0,1:T(2,128)S(1)}, s32[]{:S(2)}) async-start(s32[64,3]{0,1:T(4,128)} %copy-done.3), calls=%async_computation.8 | async-start | bytes 2048 | tf_op jit(solution)/shard_map/slice.3
  293.6 26.4 %copy-start.5 = (f32[320]{0:T(512)S(1)}, f32[320]{0:T(512)}, u32[]{:S(2)}) copy-start(f32[320]{0:T(512)} %param.19) | copy-start | bytes 3844
  296.9 67.9 %copy-start.7 = (s32[2]{0:T(128)S(1)}, s32[2]{0:T(128)}, u32[]{:S(2)}) copy-start(s32[2]{0:T(128)} %constant.170) | copy-start | bytes 28
  296.9 68.0 %copy-start.6 = (s32[2]{0:T(128)S(1)}, s32[2]{0:T(128)}, u32[]{:S(2)}) copy-start(s32[2]{0:T(128)} %constant.173) | copy-start | bytes 28
  296.9 128.7 %copy-start.1 = (bf16[512,320]{0,1:T(8,128)(2,1)S(1)}, bf16[512,320]{0,1:T(8,128)(2,1)}, u32[]{:S(2)}) copy-start(bf16[512,320]{0,1:T(8,128)(2,1)} %param.20) | copy-start | bytes 983044
  352.8 73.0 %all-to-all-start = ((bf16[64,8,320]{2,1,0:T(8,128)(2,1)}), bf16[64,8,320]{2,1,0:T(8,128)(2,1)S(1)}, u32[]{:S(2)}, u32[]{:S(2)}) async-start(bf16[64,8,320]{2,1,0:T(8,128)(2,1)} %scatter_fusion), calls=%async_computation.2 | async-start | bytes 786432 | tf_op jit(solution)/shard_map/all_to_all | solution.py:81
Sparse Core Ops, SparseCore 0:
  10.0 83.1 all-gather.7
  95.9 76.0 all-gather.9
  174.7 76.0 all-gather.5
  253.1 33.2 reduce-scatter.2
  297.0 22.8 reduce-scatter.4
